TPU v7x, 32 devices: a whole 2x2x4 slice. The times are simulated.
32 devices in a mesh: dp: 16 (over z, y, x), mp: 2 (over core).
Axes of the slice: x: 2, y: 2, z: 4, core: 2. Of those that a mesh axis runs over, the one named last changes fastest.
Arguments:
- gradients: float32 [16, 4, 32, 8192], P('dp', None, 'mp'), may hold values from -6 to 6
- weights: float32 [4, 32, 8192], P(None, 'mp', 'dp'), may hold values from -40 to 40
- first_moment: float32 [4, 32, 8192], P(None, 'mp', 'dp'), may hold values from -0.6 to 0.6
- second_moment: float32 [4, 32, 8192], P(None, 'mp', 'dp'), may hold values from 0.001 to 0.1
- learn_rate: float32 [4], replicated, may hold values from 0.1 to 0.5
- weight_decay: float32 [4], replicated, may hold values from 0.1 to 1
Outputs:
- new_weights: float32 [4, 32, 8192], P(None, 'mp')
- new_first: float32 [4, 32, 8192], P(None, 'mp', 'dp')
- new_second: float32 [4, 32, 8192], P(None, 'mp', 'dp')
- trust_ratio: float32 [4], replicated
All inputs are finite; a program needn't handle non-finite values.
Results may differ from a plain program's by a relative error of at most 0.000062.
Values sent between devices are 32-bit elements; how exact they have to be, the bound alone decides.
No kernel may reach another device: no remote copies, remote signals or barrier semaphores. Data moves between devices by JAX's collectives and lax.ppermute only.
A program may use at most 64 MiB of HBM per device.

v0:
```python
import jax
import jax.numpy as jnp
from jax import lax
from jax.sharding import PartitionSpec as P

STEP = 10


def shards(gradients, weights, first_moment, second_moment, learn_rate, weight_decay):
    replicas = lax.axis_size("dp")
    summed = lax.psum_scatter(gradients, "dp", scatter_dimension=3, tiled=True)[0] * (
        1.0 / replicas
    )
    new_first = 0.9 * first_moment + 0.1 * summed
    new_second = 0.999 * second_moment + 0.001 * summed * summed
    first_fix = 1.0 - 0.9**STEP
    second_fix = 1.0 - 0.999**STEP
    update = (
        new_first / first_fix / (jnp.sqrt(new_second / second_fix) + 1e-06)
        + weight_decay[:, None, None] * weights
    )
    weight_sq, update_sq = lax.psum(
        (jnp.sum(weights * weights, axis=(1, 2)), jnp.sum(update * update, axis=(1, 2))),
        ("dp", "mp"),
    )
    trust_ratio = jnp.sqrt(weight_sq) / (jnp.sqrt(update_sq) + 1e-06)
    stepped = weights - (learn_rate * trust_ratio)[:, None, None] * update
    new_weights = lax.all_gather(stepped, "dp", axis=2, tiled=True)
    return (new_weights, new_first, new_second, trust_ratio)


def solution(mesh):
    in_specs = (
        P("dp", None, "mp", None),
        P(None, "mp", "dp"),
        P(None, "mp", "dp"),
        P(None, "mp", "dp"),
        P(),
        P(),
    )
    out_specs = (P(None, "mp", None), P(None, "mp", "dp"), P(None, "mp", "dp"), P())
    return jax.shard_map(shards, mesh=mesh, in_specs=in_specs, out_specs=out_specs, check_vma=False)
```

profile of v0, /device:TPU:0, one launch (start us, length us, event | category | flops | bytes accessed | tf_op | source)
XLA Modules:
  0.0 205.5 jit_solution(638651230014546051)
XLA Ops:
  7.2 0.0 copy-start
  7.2 0.0 copy-start.3
  7.2 0.0 copy-start.2
  7.2 0.0 copy-start.1
  7.2 0.0 copy-start.4
  7.2 0.0 reduce-scatter.2.cloned.1.call-start
  7.3 0.7 reduce-scatter.2.cloned.1.call-update
  7.9 0.0 all-gather.2.cloned.1.call-start
  8.0 86.7 %reduce-scatter.2.cloned.1.call-done = f32[1,4,16,512]{3,2,1,0:T(8,128)} async-done(((f32[1,4,16,8192]{3,2,1,0:T(8,128)}), f32[1,4,16,512]{3,2,1,0:T(8,128)}) %reduce-scatter.2.cloned.1.call-update) | async-done | bytes 131088 | tf_op jit(solution)/shard_map/reduce_scatter | solution.py:11
  94.7 0.0 copy-done
  94.7 0.0 copy-done.3
  94.7 0.0 copy-done.2
  94.7 0.0 copy-done.1
  94.7 1.7 multiply_reduce_fusion
  96.4 36.8 %all-reduce = (f32[4]{0:T(128)S(1)}, f32[4]{0:T(128)S(1)}) all-reduce(f32[4]{0:T(128)S(1)} %get-tuple-element.8, f32[4]{0:T(128)S(1)} %get-tuple-element.12), channel_id=1, replica_groups=mesh['dp'=16,'mp'=2] {'dp','mp'}, use_global_device_ids=true, to_apply=%region_4.0 | all-reduce | flops 8 | bytes 64 | tf_op jit(solution)/shard_map/psum | solution.py:22
  133.2 0.0 copy-done.4
  133.2 0.5 fusion
  133.7 0.7 multiply_subtract_fusion
  134.4 0.0 all-gather.2.cloned.1.call-update
  134.5 61.1 %all-gather.2.cloned.1.call-done = f32[4,16,8192]{2,1,0:T(8,128)} async-done(((f32[4,16,512]{2,1,0:T(8,128)}), f32[4,16,8192]{2,1,0:T(8,128)}) %all-gather.2.cloned.1.call-update) | async-done | bytes 2097168 | tf_op jit(solution)/shard_map/all_gather | solution.py:28
  195.6 3.1 %copy.11 = f32[4,16,8192]{2,1,0:T(8,128)} copy(f32[4,16,8192]{2,1,0:T(8,128)} %all-gather.2.cloned.1.call-done) | data formatting | bytes 4194304
Async XLA Ops:
  7.2 87.5 %copy-start = (f32[4,16,512]{2,1,0:T(8,128)S(1)}, f32[4,16,512]{2,1,0:T(8,128)}, u32[]{:S(2)}) copy-start(f32[4,16,512]{2,1,0:T(8,128)} %param.7) | copy-start | bytes 393220
  7.2 87.5 %copy-start.3 = (f32[4]{0:T(128)S(1)}, f32[4]{0:T(128)}, u32[]{:S(2)}) copy-start(f32[4]{0:T(128)} %param.11) | copy-start | bytes 52
  7.2 87.5 %copy-start.2 = (f32[4,16,512]{2,1,0:T(8,128)S(1)}, f32[4,16,512]{2,1,0:T(8,128)}, u32[]{:S(2)}) copy-start(f32[4,16,512]{2,1,0:T(8,128)} %param.9) | copy-start | bytes 393220
  7.2 87.5 %copy-start.1 = (f32[4,16,512]{2,1,0:T(8,128)S(1)}, f32[4,16,512]{2,1,0:T(8,128)}, u32[]{:S(2)}) copy-start(f32[4,16,512]{2,1,0:T(8,128)} %param.8) | copy-start | bytes 393220
  7.2 126.0 %copy-start.4 = (f32[4]{0:T(128)S(1)}, f32[4]{0:T(128)}, u32[]{:S(2)}) copy-start(f32[4]{0:T(128)} %param.10) | copy-start | bytes 52
  7.2 87.4 %reduce-scatter.2.cloned.1.call-start = ((), (), s32[]{:S(2)}) async-start(), calls=%async_computation.1 | async-start | bytes 2228224 | tf_op jit(solution)/shard_map/reduce_scatter | solution.py:11
  7.9 187.6 %all-gather.2.cloned.1.call-start = ((), (), s32[]{:S(2)}) async-start(), calls=%async_computation.2 | async-start | bytes 2228224 | tf_op jit(solution)/shard_map/all_gather | solution.py:28
Sparse Core Ops, SparseCore 0:
  10.3 84.3 reduce-scatter.1
  134.6 60.9 all-gather.1
where the time goes:
time: 206 us; the launch traced here: 205 us
  waiting for transfers between devices  148 us (72%)
  blocking collectives  36.8 us (18%)
  between operations  14.1 us (7%)
  local copies, waits for them, and re-layouts  3.08 us (1%)
  other arithmetic  2.97 us (1%)
    reduce_scatter x1, waiting for transfers between devices, shards(): lax.psum_scatter(gradients, 'dp', scatter_dimension=3, tiled=True)[0]  86.7 us
    all_gather x1, waiting for transfers between devices, shards(): new_weights = lax.all_gather(stepped, 'dp', axis=2, tiled=True)  61.1 us
    psum x1, blocking collectives, shards(): lax.psum((jnp.sum(weights * weights, axis=(1, 2)), jnp.sum(update * updat...  36.8 us
  transfers between devices with their start and end apart: 2, of which 2 were waited for; matrix products, arithmetic and copies ran while one was open for 0% of the time, Pallas kernels for 0%

commit v1 on v0

--- a/solution.py
+++ b/solution.py
@@ -25,7 +25,13 @@
     )
     trust_ratio = jnp.sqrt(weight_sq) / (jnp.sqrt(update_sq) + 1e-06)
     stepped = weights - (learn_rate * trust_ratio)[:, None, None] * update
-    new_weights = lax.all_gather(stepped, "dp", axis=2, tiled=True)
+    size = lax.axis_size("dp")
+    held, blocks = (stepped, [stepped])
+    for _ in range(size - 1):
+        held = lax.ppermute(held, "dp", [(i, (i + 1) % size) for i in range(size)])
+        blocks.insert(0, held)
+    flat = jnp.concatenate(blocks, axis=2)
+    new_weights = jnp.roll(flat, (lax.axis_index("dp") + 1) * stepped.shape[2], axis=2)
     return (new_weights, new_first, new_second, trust_ratio)
 
 

time: 206 us -> 277 us (1.34)
  waiting for transfers between devices: 148 us -> 217 us
    ppermute x0 -> x15, waiting for transfers between devices: none -> 130 us  [shards(): held = lax.ppermute(held, 'dp', [(i, (i + 1) % size) for i in range(size)])]
    all_gather x1 -> x0, waiting for transfers between devices: 61.1 us -> none  [shards(): new_weights = lax.all_gather(stepped, 'dp', axis=2, tiled=True)]
  transfers between devices with their start and end apart: 2 -> 16, of which waited for: 2 -> 16; matrix products, arithmetic and copies ran while one was open for 0% -> 0% of each run, Pallas kernels for 0% -> 0%
where the time goes in v1:
time: 277 us
  waiting for transfers between devices  217 us (78%)
  blocking collectives  36.8 us (13%)
  between operations  14.3 us (5%)
  other arithmetic  4.08 us (1%)
    ppermute x15, waiting for transfers between devices, shards(): held = lax.ppermute(held, 'dp', [(i, (i + 1) % size) for i in range(size)])  130 us
    reduce_scatter x1, waiting for transfers between devices, shards(): lax.psum_scatter(gradients, 'dp', scatter_dimension=3, tiled=True)[0]  86.7 us
    psum x1, blocking collectives, shards(): lax.psum((jnp.sum(weights * weights, axis=(1, 2)), jnp.sum(update * updat...  36.8 us
  transfers between devices with their start and end apart: 16, of which 16 were waited for; matrix products, arithmetic and copies ran while one was open for 0% of the time, Pallas kernels for 0%

profile of v1, /device:TPU:0, one launch (start us, length us, event | category | flops | bytes accessed | tf_op | source)
XLA Modules:
  0.0 276.5 jit_solution(16021461847107393293)
XLA Ops:
  7.2 0.0 reduce-scatter.2.cloned.1.call-start
  7.2 0.7 reduce-scatter.2.cloned.1.call-update
  7.9 86.7 %reduce-scatter.2.cloned.1.call-done = f32[1,4,16,512]{3,2,1,0:T(8,128)} async-done(((f32[1,4,16,8192]{3,2,1,0:T(8,128)}), f32[1,4,16,512]{3,2,1,0:T(8,128)}) %reduce-scatter.2.cloned.1.call-update) | async-done | bytes 131088 | tf_op jit(solution)/shard_map/reduce_scatter | solution.py:11
  94.6 1.9 multiply_reduce_fusion
  96.5 36.8 %all-reduce = (f32[4]{0:T(128)S(1)}, f32[4]{0:T(128)S(1)}) all-reduce(f32[4]{0:T(128)S(1)} %get-tuple-element.8, f32[4]{0:T(128)S(1)} %get-tuple-element.12), channel_id=1, replica_groups=mesh['dp'=16,'mp'=2] {'dp','mp'}, use_global_device_ids=true, to_apply=%region_4.0 | all-reduce | flops 8 | bytes 64 | tf_op jit(solution)/shard_map/psum | solution.py:22
  133.3 1.2 fusion
  134.5 1.0 multiply_subtract_fusion
  135.5 2.3 collective-permute-start
  137.8 6.3 %collective-permute-done = f32[4,16,512]{2,1,0:T(8,128)S(1)} collective-permute-done((f32[4,16,512]{2,1,0:T(8,128)S(1)}, f32[4,16,512]{2,1,0:T(8,128)S(1)}, u32[]{:S(2)}, u32[]{:S(2)}) %collective-permute-start) | collective-permute-done | bytes 131104 | tf_op jit(solution)/shard_map/ppermute | solution.py:31
  144.1 8.6 %collective-permute-done.1 = f32[4,16,512]{2,1,0:T(8,128)S(1)} collective-permute-done((f32[4,16,512]{2,1,0:T(8,128)S(1)}, f32[4,16,512]{2,1,0:T(8,128)S(1)}, u32[]{:S(2)}, u32[]{:S(2)}) %collective-permute-start.1) | collective-permute-done | bytes 131104 | tf_op jit(solution)/shard_map/ppermute | solution.py:31
  152.7 8.6 %collective-permute-done.2 = f32[4,16,512]{2,1,0:T(8,128)S(1)} collective-permute-done((f32[4,16,512]{2,1,0:T(8,128)S(1)}, f32[4,16,512]{2,1,0:T(8,128)S(1)}, u32[]{:S(2)}, u32[]{:S(2)}) %collective-permute-start.2) | collective-permute-done | bytes 131104 | tf_op jit(solution)/shard_map/ppermute | solution.py:31
  161.2 8.6 %collective-permute-done.3 = f32[4,16,512]{2,1,0:T(8,128)S(1)} collective-permute-done((f32[4,16,512]{2,1,0:T(8,128)S(1)}, f32[4,16,512]{2,1,0:T(8,128)S(1)}, u32[]{:S(2)}, u32[]{:S(2)}) %collective-permute-start.3) | collective-permute-done | bytes 131104 | tf_op jit(solution)/shard_map/ppermute | solution.py:31
  169.8 9.1 %collective-permute-done.4 = f32[4,16,512]{2,1,0:T(8,128)S(1)} collective-permute-done((f32[4,16,512]{2,1,0:T(8,128)S(1)}, f32[4,16,512]{2,1,0:T(8,128)S(1)}, u32[]{:S(2)}, u32[]{:S(2)}) %collective-permute-start.4) | collective-permute-done | bytes 131104 | tf_op jit(solution)/shard_map/ppermute | solution.py:31
  178.9 9.7 %collective-permute-done.5 = f32[4,16,512]{2,1,0:T(8,128)S(1)} collective-permute-done((f32[4,16,512]{2,1,0:T(8,128)S(1)}, f32[4,16,512]{2,1,0:T(8,128)S(1)}, u32[]{:S(2)}, u32[]{:S(2)}) %collective-permute-start.5) | collective-permute-done | bytes 131104 | tf_op jit(solution)/shard_map/ppermute | solution.py:31
  188.6 8.8 %collective-permute-done.6 = f32[4,16,512]{2,1,0:T(8,128)S(1)} collective-permute-done((f32[4,16,512]{2,1,0:T(8,128)S(1)}, f32[4,16,512]{2,1,0:T(8,128)S(1)}, u32[]{:S(2)}, u32[]{:S(2)}) %collective-permute-start.6) | collective-permute-done | bytes 131104 | tf_op jit(solution)/shard_map/ppermute | solution.py:31
  197.4 8.6 %collective-permute-done.7 = f32[4,16,512]{2,1,0:T(8,128)S(1)} collective-permute-done((f32[4,16,512]{2,1,0:T(8,128)S(1)}, f32[4,16,512]{2,1,0:T(8,128)S(1)}, u32[]{:S(2)}, u32[]{:S(2)}) %collective-permute-start.7) | collective-permute-done | bytes 131104 | tf_op jit(solution)/shard_map/ppermute | solution.py:31
  206.0 8.6 %collective-permute-done.8 = f32[4,16,512]{2,1,0:T(8,128)S(1)} collective-permute-done((f32[4,16,512]{2,1,0:T(8,128)S(1)}, f32[4,16,512]{2,1,0:T(8,128)S(1)}, u32[]{:S(2)}, u32[]{:S(2)}) %collective-permute-start.8) | collective-permute-done | bytes 131104 | tf_op jit(solution)/shard_map/ppermute | solution.py:31
  214.5 8.6 %collective-permute-done.9 = f32[4,16,512]{2,1,0:T(8,128)S(1)} collective-permute-done((f32[4,16,512]{2,1,0:T(8,128)S(1)}, f32[4,16,512]{2,1,0:T(8,128)S(1)}, u32[]{:S(2)}, u32[]{:S(2)}) %collective-permute-start.9) | collective-permute-done | bytes 131104 | tf_op jit(solution)/shard_map/ppermute | solution.py:31
  223.1 8.6 %collective-permute-done.10 = f32[4,16,512]{2,1,0:T(8,128)S(1)} collective-permute-done((f32[4,16,512]{2,1,0:T(8,128)S(1)}, f32[4,16,512]{2,1,0:T(8,128)S(1)}, u32[]{:S(2)}, u32[]{:S(2)}) %collective-permute-start.10) | collective-permute-done | bytes 131104 | tf_op jit(solution)/shard_map/ppermute | solution.py:31
  231.7 9.1 %collective-permute-done.11 = f32[4,16,512]{2,1,0:T(8,128)S(1)} collective-permute-done((f32[4,16,512]{2,1,0:T(8,128)S(1)}, f32[4,16,512]{2,1,0:T(8,128)S(1)}, u32[]{:S(2)}, u32[]{:S(2)}) %collective-permute-start.11) | collective-permute-done | bytes 131104 | tf_op jit(solution)/shard_map/ppermute | solution.py:31
  240.8 9.6 %collective-permute-done.12 = f32[4,16,512]{2,1,0:T(8,128)S(1)} collective-permute-done((f32[4,16,512]{2,1,0:T(8,128)S(1)}, f32[4,16,512]{2,1,0:T(8,128)S(1)}, u32[]{:S(2)}, u32[]{:S(2)}) %collective-permute-start.12) | collective-permute-done | bytes 131104 | tf_op jit(solution)/shard_map/ppermute | solution.py:31
  250.5 8.6 %collective-permute-done.13 = f32[4,16,512]{2,1,0:T(8,128)S(1)} collective-permute-done((f32[4,16,512]{2,1,0:T(8,128)S(1)}, f32[4,16,512]{2,1,0:T(8,128)S(1)}, u32[]{:S(2)}, u32[]{:S(2)}) %collective-permute-start.13) | collective-permute-done | bytes 131104 | tf_op jit(solution)/shard_map/ppermute | solution.py:31
  259.0 8.6 %collective-permute-done.14 = f32[4,16,512]{2,1,0:T(8,128)S(1)} collective-permute-done((f32[4,16,512]{2,1,0:T(8,128)S(1)}, f32[4,16,512]{2,1,0:T(8,128)S(1)}, u32[]{:S(2)}, u32[]{:S(2)}) %collective-permute-start.14) | collective-permute-done | bytes 131104 | tf_op jit(solution)/shard_map/ppermute | solution.py:31
  268.2 1.5 constant_dynamic-slice_fusion
  (46 shorter events, 0.4 us)
Async XLA Ops:
  7.2 87.4 %reduce-scatter.2.cloned.1.call-start = ((), (), s32[]{:S(2)}) async-start(), calls=%async_computation.1 | async-start | bytes 2228224 | tf_op jit(solution)/shard_map/reduce_scatter | solution.py:11
  135.5 8.6 %collective-permute-start = (f32[4,16,512]{2,1,0:T(8,128)S(1)}, f32[4,16,512]{2,1,0:T(8,128)S(1)}, u32[]{:S(2)}, u32[]{:S(2)}) collective-permute-start(f32[4,16,512]{2,1,0:T(8,128)S(1)} %multiply_subtract_fusion), channel_id=1, source_target_pairs={{0,2},{2,4},{4,6},{6,8},{8,10},{10,12},{12,14},{14,16},{16,18},{18... | collective-permute-start | bytes 393224 | tf_op jit(solution)/shard_map/ppermute | solution.py:31
  144.1 8.6 %collective-permute-start.1 = (f32[4,16,512]{2,1,0:T(8,128)S(1)}, f32[4,16,512]{2,1,0:T(8,128)S(1)}, u32[]{:S(2)}, u32[]{:S(2)}) collective-permute-start(f32[4,16,512]{2,1,0:T(8,128)S(1)} %collective-permute-done), channel_id=1, source_target_pairs={{0,2},{2,4},{4,6},{6,8},{8,10},{10,12},{12,14},{14,16},{16,18},{18... | collective-permute-start | bytes 393224 | tf_op jit(solution)/shard_map/ppermute | solution.py:31
  152.7 8.6 %collective-permute-start.2 = (f32[4,16,512]{2,1,0:T(8,128)S(1)}, f32[4,16,512]{2,1,0:T(8,128)S(1)}, u32[]{:S(2)}, u32[]{:S(2)}) collective-permute-start(f32[4,16,512]{2,1,0:T(8,128)S(1)} %collective-permute-done.1), channel_id=1, source_target_pairs={{0,2},{2,4},{4,6},{6,8},{8,10},{10,12},{12,14},{14,16},{16,18},{18... | collective-permute-start | bytes 393224 | tf_op jit(solution)/shard_map/ppermute | solution.py:31
  161.2 8.6 %collective-permute-start.3 = (f32[4,16,512]{2,1,0:T(8,128)S(1)}, f32[4,16,512]{2,1,0:T(8,128)S(1)}, u32[]{:S(2)}, u32[]{:S(2)}) collective-permute-start(f32[4,16,512]{2,1,0:T(8,128)S(1)} %collective-permute-done.2), channel_id=1, source_target_pairs={{0,2},{2,4},{4,6},{6,8},{8,10},{10,12},{12,14},{14,16},{16,18},{18... | collective-permute-start | bytes 393224 | tf_op jit(solution)/shard_map/ppermute | solution.py:31
  169.8 9.1 %collective-permute-start.4 = (f32[4,16,512]{2,1,0:T(8,128)S(1)}, f32[4,16,512]{2,1,0:T(8,128)S(1)}, u32[]{:S(2)}, u32[]{:S(2)}) collective-permute-start(f32[4,16,512]{2,1,0:T(8,128)S(1)} %collective-permute-done.3), channel_id=1, source_target_pairs={{0,2},{2,4},{4,6},{6,8},{8,10},{10,12},{12,14},{14,16},{16,18},{18... | collective-permute-start | bytes 393224 | tf_op jit(solution)/shard_map/ppermute | solution.py:31
  178.9 9.7 %collective-permute-start.5 = (f32[4,16,512]{2,1,0:T(8,128)S(1)}, f32[4,16,512]{2,1,0:T(8,128)S(1)}, u32[]{:S(2)}, u32[]{:S(2)}) collective-permute-start(f32[4,16,512]{2,1,0:T(8,128)S(1)} %collective-permute-done.4), channel_id=1, source_target_pairs={{0,2},{2,4},{4,6},{6,8},{8,10},{10,12},{12,14},{14,16},{16,18},{18... | collective-permute-start | bytes 393224 | tf_op jit(solution)/shard_map/ppermute | solution.py:31
  188.6 8.8 %collective-permute-start.6 = (f32[4,16,512]{2,1,0:T(8,128)S(1)}, f32[4,16,512]{2,1,0:T(8,128)S(1)}, u32[]{:S(2)}, u32[]{:S(2)}) collective-permute-start(f32[4,16,512]{2,1,0:T(8,128)S(1)} %collective-permute-done.5), channel_id=1, source_target_pairs={{0,2},{2,4},{4,6},{6,8},{8,10},{10,12},{12,14},{14,16},{16,18},{18... | collective-permute-start | bytes 393224 | tf_op jit(solution)/shard_map/ppermute | solution.py:31
  197.4 8.6 %collective-permute-start.7 = (f32[4,16,512]{2,1,0:T(8,128)S(1)}, f32[4,16,512]{2,1,0:T(8,128)S(1)}, u32[]{:S(2)}, u32[]{:S(2)}) collective-permute-start(f32[4,16,512]{2,1,0:T(8,128)S(1)} %collective-permute-done.6), channel_id=1, source_target_pairs={{0,2},{2,4},{4,6},{6,8},{8,10},{10,12},{12,14},{14,16},{16,18},{18... | collective-permute-start | bytes 393224 | tf_op jit(solution)/shard_map/ppermute | solution.py:31
  206.0 8.6 %collective-permute-start.8 = (f32[4,16,512]{2,1,0:T(8,128)S(1)}, f32[4,16,512]{2,1,0:T(8,128)S(1)}, u32[]{:S(2)}, u32[]{:S(2)}) collective-permute-start(f32[4,16,512]{2,1,0:T(8,128)S(1)} %collective-permute-done.7), channel_id=1, source_target_pairs={{0,2},{2,4},{4,6},{6,8},{8,10},{10,12},{12,14},{14,16},{16,18},{18... | collective-permute-start | bytes 393224 | tf_op jit(solution)/shard_map/ppermute | solution.py:31
  214.5 8.6 %collective-permute-start.9 = (f32[4,16,512]{2,1,0:T(8,128)S(1)}, f32[4,16,512]{2,1,0:T(8,128)S(1)}, u32[]{:S(2)}, u32[]{:S(2)}) collective-permute-start(f32[4,16,512]{2,1,0:T(8,128)S(1)} %collective-permute-done.8), channel_id=1, source_target_pairs={{0,2},{2,4},{4,6},{6,8},{8,10},{10,12},{12,14},{14,16},{16,18},{18... | collective-permute-start | bytes 393224 | tf_op jit(solution)/shard_map/ppermute | solution.py:31
  223.1 8.6 %collective-permute-start.10 = (f32[4,16,512]{2,1,0:T(8,128)S(1)}, f32[4,16,512]{2,1,0:T(8,128)S(1)}, u32[]{:S(2)}, u32[]{:S(2)}) collective-permute-start(f32[4,16,512]{2,1,0:T(8,128)S(1)} %collective-permute-done.9), channel_id=1, source_target_pairs={{0,2},{2,4},{4,6},{6,8},{8,10},{10,12},{12,14},{14,16},{16,18},{18... | collective-permute-start | bytes 393224 | tf_op jit(solution)/shard_map/ppermute | solution.py:31
  231.7 9.1 %collective-permute-start.11 = (f32[4,16,512]{2,1,0:T(8,128)S(1)}, f32[4,16,512]{2,1,0:T(8,128)S(1)}, u32[]{:S(2)}, u32[]{:S(2)}) collective-permute-start(f32[4,16,512]{2,1,0:T(8,128)S(1)} %collective-permute-done.10), channel_id=1, source_target_pairs={{0,2},{2,4},{4,6},{6,8},{8,10},{10,12},{12,14},{14,16},{16,18},{18... | collective-permute-start | bytes 393224 | tf_op jit(solution)/shard_map/ppermute | solution.py:31
  240.8 9.6 %collective-permute-start.12 = (f32[4,16,512]{2,1,0:T(8,128)S(1)}, f32[4,16,512]{2,1,0:T(8,128)S(1)}, u32[]{:S(2)}, u32[]{:S(2)}) collective-permute-start(f32[4,16,512]{2,1,0:T(8,128)S(1)} %collective-permute-done.11), channel_id=1, source_target_pairs={{0,2},{2,4},{4,6},{6,8},{8,10},{10,12},{12,14},{14,16},{16,18},{18... | collective-permute-start | bytes 393224 | tf_op jit(solution)/shard_map/ppermute | solution.py:31
  250.5 8.6 %collective-permute-start.13 = (f32[4,16,512]{2,1,0:T(8,128)S(1)}, f32[4,16,512]{2,1,0:T(8,128)S(1)}, u32[]{:S(2)}, u32[]{:S(2)}) collective-permute-start(f32[4,16,512]{2,1,0:T(8,128)S(1)} %collective-permute-done.12), channel_id=1, source_target_pairs={{0,2},{2,4},{4,6},{6,8},{8,10},{10,12},{12,14},{14,16},{16,18},{18... | collective-permute-start | bytes 393224 | tf_op jit(solution)/shard_map/ppermute | solution.py:31
  259.0 8.6 %collective-permute-start.14 = (f32[4,16,512]{2,1,0:T(8,128)S(1)}, f32[4,16,512]{2,1,0:T(8,128)S(1)}, u32[]{:S(2)}, u32[]{:S(2)}) collective-permute-start(f32[4,16,512]{2,1,0:T(8,128)S(1)} %collective-permute-done.13), channel_id=1, source_target_pairs={{0,2},{2,4},{4,6},{6,8},{8,10},{10,12},{12,14},{14,16},{16,18},{18... | collective-permute-start | bytes 393224 | tf_op jit(solution)/shard_map/ppermute | solution.py:31
Sparse Core Ops, SparseCore 0:
  10.2 84.3 reduce-scatter.1
